TPU v7x, 512 devices: a whole 4x8x8 slice. The times are simulated.
512 devices in a mesh: prow: 16 (over x, z_hi), pcol: 32 (over z_lo, y, core).
Axes of the slice: x: 4, y: 8, z: 8 (z_hi: 4, z_lo: 2; z = z_hi * 2 + z_lo), core: 2. Of those that a mesh axis runs over, the one named last changes fastest.
Arguments:
- ancestor_inverse: bfloat16 [24576, 24576], P('pcol', 'prow'), may hold values from -6 to 6
- lower_panel: bfloat16 [24576, 1024], P(('prow', 'pcol')), may hold values from -0.3125 to 0.3125
- pivot_inverse: float32 [256, 1024], P('pcol', 'prow'), may hold values from -6 to 6
- struct_list: int32 [4, 48], replicated, may hold values from -1 to 95, as said below
Outputs:
- off_inverse: bfloat16 [24576, 1024], P('pcol', 'prow')
- diag_inverse: float32 [256, 1024], P('pcol', 'prow')
Inputs may be any that keep to these rules, and one draw needn't show every extreme that they name: `struct_list`: each row lists distinct ancestor supernodes first, all within 48 cyclically consecutive ancestor numbers, then entries -1; every row has at least one ancestor and some row lists 48.
All inputs are finite; a program needn't handle non-finite values.
Results may differ from a plain program's by a relative error of at most 0.001.
Values may be sent and summed in bfloat16 or wider, within the bound.
A program may use at most 64 MiB of HBM per device.

v0:
```python
import jax
import jax.numpy as jnp
from jax import lax
from jax.sharding import PartitionSpec as P

B = 256
NK = 4


def from_root(value, axis, root):
    mine = lax.axis_index(axis) == root
    return lax.psum(jnp.where(mine, value, jnp.zeros_like(value)), axis)


def membership(struct_list, ancestor_ids):
    listed = struct_list[:, :, None] == ancestor_ids[None, None, :]
    return jnp.transpose(jnp.any(listed, axis=1))


def body(ancestor_inverse, lower_panel, pivot_inverse, struct_list):
    row_count = ancestor_inverse.shape[0] // B
    col_count = ancestor_inverse.shape[1] // B
    grid_rows = lax.axis_size("prow")
    prow_index = lax.axis_index("prow")
    pcol_index = lax.axis_index("pcol")
    col_share = NK * B // grid_rows
    gathered = lax.all_gather(lower_panel, "pcol", axis=0, tiled=True)
    col_ids = prow_index * col_count + jnp.arange(col_count, dtype=jnp.int32)
    row_ids = pcol_index * row_count + jnp.arange(row_count, dtype=jnp.int32)
    member_cols = membership(struct_list, col_ids)
    member_rows = membership(struct_list, row_ids)
    scaled = gathered.reshape(col_count, B, NK, B) * member_cols[:, None, :, None].astype(
        jnp.bfloat16
    )
    masked = scaled.reshape(col_count * B, NK * B)
    partial_value = -jnp.dot(ancestor_inverse, masked, preferred_element_type=jnp.float32)
    share_sum = lax.psum_scatter(partial_value, "prow", scatter_dimension=1, tiled=True)
    columns = prow_index * col_share + jnp.arange(col_share, dtype=jnp.int32)
    block_of = columns // B
    one_hot = block_of[:, None] == jnp.arange(NK, dtype=jnp.int32)[None, :]
    row_mask = jnp.any(member_rows[:, None, :] & one_hot[None, :, :], axis=2).astype(jnp.float32)
    off_share = (share_sum.reshape(row_count, B, col_share) * row_mask[:, None, :]).reshape(
        row_count * B, col_share
    )
    off_inverse = off_share.astype(jnp.bfloat16)
    block_count = max(col_share // B, 1)
    column_width = col_share // block_count
    offset_blocks = pcol_index * row_count % col_count
    root_row = pcol_index * row_count // col_count
    piece = lax.dynamic_slice_in_dim(masked, offset_blocks * B, row_count * B, 0)
    lower_rows = from_root(piece, "prow", root_row)
    first_block = prow_index * col_share // B
    lower_slice = lax.dynamic_slice_in_dim(lower_rows, first_block * B, block_count * B, 1)
    lower_blocks = lower_slice.astype(jnp.float32).reshape(row_count * B, block_count, B)
    off_blocks = off_share.reshape(row_count * B, block_count, column_width)
    diag_term = jnp.einsum(
        "ikr,ikc->rkc", lower_blocks, off_blocks, precision=lax.Precision.HIGHEST
    ).reshape(B, col_share)
    diag_share = lax.psum_scatter(diag_term, "pcol", scatter_dimension=0, tiled=True)
    diag_inverse = pivot_inverse - diag_share
    return (off_inverse, diag_inverse)


def solution(mesh):
    placed = (P("pcol", "prow"), P(("prow", "pcol"), None), P("pcol", "prow"), P())
    return jax.shard_map(
        body,
        mesh=mesh,
        in_specs=placed,
        out_specs=(P("pcol", "prow"), P("pcol", "prow")),
        check_vma=False,
    )
```

profile of v0, /device:TPU:25, one launch (start us, length us, event | category | flops | bytes accessed | tf_op | source)
XLA Modules:
  0.0 580.3 jit_solution(7268216275840129706)
XLA Ops:
  7.2 0.7 all-gather.2.cloned.1.call-update
  8.0 0.9 compare_reduce_fusion
  8.9 0.9 mul.43
  9.8 2.5 copy.20
  12.3 69.3 %all-gather.2.cloned.1.call-done = bf16[1536,1024]{1,0:T(8,128)(2,1)} async-done(((bf16[48,1024]{1,0:T(8,128)(2,1)}), bf16[1536,1024]{1,0:T(8,128)(2,1)}) %all-gather.2.cloned.1.call-update) | async-done | bytes 3145744 | tf_op jit(solution)/shard_map/all_gather | solution.py:27
  81.6 4.4 mul.45
  86.0 1.7 copy-done.1
  87.7 1.6 dynamic-slice_select_fusion
  89.3 0.0 reduce-scatter.3.cloned.1.call-start
  89.4 6.2 %negate_bitcast_fusion = f32[768,1024]{0,1:T(8,128)} fusion(bf16[1536,1024]{1,0:T(8,128)(2,1)} %copy-done.1, bf16[768,1536]{1,0:T(8,128)(2,1)S(1)} %copy-done), kind=kOutput, calls=%fused_computation | convolution fusion | flops 2416705536 | bytes 8650752 | tf_op jit(solution)/shard_map/dot_general | solution.py:36
  95.7 0.6 copy-done.2
  96.3 0.2 compare_reduce_fusion.1
  96.5 0.1 and_reduce_fusion
  96.6 0.1 copy.15
  96.7 0.1 mul.48
  96.9 0.1 copy.16
  97.0 1.3 dynamic-slice
  98.9 161.5 %all-reduce.4.cloned.1.call-done = bf16[768,1024]{1,0:T(8,128)(2,1)} async-done(((bf16[768,1024]{1,0:T(8,128)(2,1)}), bf16[768,1024]{1,0:T(8,128)(2,1)}) %all-reduce.4.cloned.1.call-update) | async-done | bytes 1572880 | tf_op jit(solution)/shard_map/psum | solution.py:12
  260.4 109.3 %reduce-scatter.3.cloned.1.call-done = f32[768,64]{0,1:T(8,128)} async-done(((f32[768,1024]{0,1:T(8,128)}), f32[768,64]{0,1:T(8,128)}) %reduce-scatter.3.cloned.1.call-update) | async-done | bytes 196624 | tf_op jit(solution)/shard_map/reduce_scatter | solution.py:37
  369.7 2.0 convolution_bitcast_fusion
  371.8 1.6 multiply_convert_fusion
  373.4 198.9 %all-reduce.6.cloned.1.call-done = f32[256,64]{0,1:T(8,128)} async-done(((f32[256,64]{0,1:T(8,128)}), f32[256,64]{0,1:T(8,128)}) %all-reduce.6.cloned.1.call-update) | async-done | bytes 65552
  572.3 0.8 dynamic-slice_subtract_fusion
  573.1 0.7 copy.17
  (19 shorter events, 0.3 us)
Async XLA Ops:
  7.2 82.2 %copy-start = (bf16[768,1536]{1,0:T(8,128)(2,1)S(1)}, bf16[768,1536]{1,0:T(8,128)(2,1)}, u32[]{:S(2)}) copy-start(bf16[768,1536]{1,0:T(8,128)(2,1)} %param.4) | copy-start | bytes 7077892
  7.2 74.5 %all-gather.2.cloned.1.call-start = ((), (), s32[]{:S(2)}) async-start(), calls=%async_computation.1 | async-start | bytes 3244032 | tf_op jit(solution)/shard_map/all_gather | solution.py:27
  7.9 252.5 %all-reduce.4.cloned.1.call-start = ((), (), s32[]{:S(2)}) async-start(), calls=%async_computation.3 | async-start | bytes 3145728 | tf_op jit(solution)/shard_map/psum | solution.py:12
  86.0 1.7 copy-start.1
  89.3 280.4 %reduce-scatter.3.cloned.1.call-start = ((), (), s32[]{:S(2)}) async-start(), calls=%async_computation.2 | async-start | bytes 3342336 | tf_op jit(solution)/shard_map/reduce_scatter | solution.py:37
  95.6 0.7 copy-start.2
  95.6 1.3 copy-start.3
  95.7 476.6 %all-reduce.6.cloned.1.call-start = ((), (), s32[]{:S(2)}) async-start(), calls=%async_computation.4 | async-start | bytes 131072
Sparse Core Ops, SparseCore 0:
  10.1 71.4 all-gather.1
  89.4 170.8 all-reduce.3
  264.6 105.0 reduce-scatter.2
  372.5 199.7 all-reduce.5
where the time goes:
time: 581 us; the launch traced here: 580 us
  waiting for transfers between devices  540 us (93%)
  between operations  14.6 us (3%)
  other arithmetic  9.68 us (2%)
  matrix products  8.29 us (1%)
  local copies, waits for them, and re-layouts  7.86 us (1%)
    unnamed x5, waiting for transfers between devices  200 us
    psum x1, waiting for transfers between devices, from_root(): return lax.psum(jnp.where(mine, value, jnp.zeros_like(value)), axis)  161 us
    reduce_scatter x1, waiting for transfers between devices, body(): lax.psum_scatter(partial_value, 'prow', scatter_dimension=1, tiled=True)  109 us
    all_gather x1, waiting for transfers between devices, body(): gathered = lax.all_gather(lower_panel, 'pcol', axis=0, tiled=True)  69.3 us
  transfers between devices with their start and end apart: 4, of which 4 were waited for; matrix products, arithmetic and copies ran while one was open for 2% of the time, Pallas kernels for 0%

commit v1 on v0

--- a/solution.py
+++ b/solution.py
@@ -9,7 +9,7 @@
 
 def from_root(value, axis, root):
     mine = lax.axis_index(axis) == root
-    return lax.psum(jnp.where(mine, value, jnp.zeros_like(value)), axis)
+    return jnp.sum(lax.all_gather(jnp.where(mine, value, jnp.zeros_like(value)), axis), axis=0)
 
 
 def membership(struct_list, ancestor_ids):

time: 581 us -> 695 us (1.20)
  waiting for transfers between devices: 540 us -> 638 us
  other arithmetic: 9.68 us -> 24.6 us
    all_gather x0 -> x1, waiting for transfers between devices: none -> 281 us  [from_root(): lax.all_gather(jnp.where(mine, value, jnp.zeros_like(value)), axis)]
    psum x1 -> x0, waiting for transfers between devices: 161 us -> none  [from_root(): return lax.psum(jnp.where(mine, value, jnp.zeros_like(value)), axis)]
    reduce_scatter x1, waiting for transfers between devices: 109 us -> 88.5 us  [body(): lax.psum_scatter(partial_value, 'prow', scatter_dimension=1, tiled=True)]
    reduce_sum x0 -> x1, other arithmetic: none -> 15 us  [from_root(): jnp.sum(lax.all_gather(jnp.where(mine, value, jnp.zeros_like(value)), axi...]
  transfers between devices with their start and end apart: 4 -> 4, of which waited for: 4 -> 4; matrix products, arithmetic and copies ran while one was open for 2% -> 4% of each run, Pallas kernels for 0% -> 0%
where the time goes in v1:
time: 695 us; the launch traced here: 694 us
  waiting for transfers between devices  638 us (92%)
  other arithmetic  24.6 us (4%)
  between operations  14.6 us (2%)
  matrix products  8.35 us (1%)
  local copies, waits for them, and re-layouts  7.94 us (1%)
    all_gather x1, waiting for transfers between devices, from_root(): lax.all_gather(jnp.where(mine, value, jnp.zeros_like(value)), axis)  281 us
    unnamed x5, waiting for transfers between devices  200 us
    reduce_scatter x1, waiting for transfers between devices, body(): lax.psum_scatter(partial_value, 'prow', scatter_dimension=1, tiled=True)  88.5 us
    all_gather x1, waiting for transfers between devices, body(): gathered = lax.all_gather(lower_panel, 'pcol', axis=0, tiled=True)  69.3 us
    reduce_sum x1, other arithmetic, from_root(): jnp.sum(lax.all_gather(jnp.where(mine, value, jnp.zeros_like(value)), axi...  15 us
  transfers between devices with their start and end apart: 4, of which 4 were waited for; matrix products, arithmetic and copies ran while one was open for 4% of the time, Pallas kernels for 0%

profile of v1, /device:TPU:25, one launch (start us, length us, event | category | flops | bytes accessed | tf_op | source)
XLA Modules:
  0.0 694.1 jit_solution(2778156397415640099)
XLA Ops:
  7.2 0.7 all-gather.4.cloned.1.call-update
  8.0 0.9 compare_reduce_fusion
  9.0 0.9 mul.43
  9.8 2.5 copy.20
  12.3 69.3 %all-gather.4.cloned.1.call-done = bf16[1536,1024]{1,0:T(8,128)(2,1)} async-done(((bf16[48,1024]{1,0:T(8,128)(2,1)}), bf16[1536,1024]{1,0:T(8,128)(2,1)}) %all-gather.4.cloned.1.call-update) | async-done | bytes 3145744 | tf_op jit(solution)/shard_map/all_gather | solution.py:27
  81.6 4.4 mul.45
  86.0 1.7 copy-done.1
  87.8 1.6 dynamic-slice_select_fusion
  89.4 6.3 negate_bitcast_fusion
  95.8 0.6 copy-done.2
  96.4 0.2 compare_reduce_fusion.1
  96.6 0.1 and_reduce_fusion
  96.7 0.1 copy.15
  96.8 0.1 copy.16
  96.9 0.1 mul.48
  97.1 1.3 dynamic-slice
  99.0 281.1 %all-gather.6.cloned.1.call-done = bf16[12288,1024]{1,0:T(8,128)(2,1)} async-done(((bf16[768,1024]{1,0:T(8,128)(2,1)}), bf16[12288,1024]{1,0:T(8,128)(2,1)}) %all-gather.6.cloned.1.call-update) | async-done | bytes 25165840 | tf_op jit(solution)/shard_map/all_gather | solution.py:12
  380.1 15.0 %reduce_sum.12 = bf16[768,1024]{1,0:T(8,128)(2,1)} reduce(bf16[16,768,1024]{2,1,0:T(8,128)(2,1)} %bitcast.24, bf16[]{:T(256)} %constant.61.clone.1), dimensions={0}, to_apply=%region_4.5 | reduce | flops 11796480 | bytes 26738690 | tf_op jit(solution)/shard_map/reduce_sum | solution.py:12
  395.1 88.5 %reduce-scatter.3.cloned.1.call-done = f32[768,64]{0,1:T(8,128)} async-done(((f32[768,1024]{0,1:T(8,128)}), f32[768,64]{0,1:T(8,128)}) %reduce-scatter.3.cloned.1.call-update) | async-done | bytes 196624 | tf_op jit(solution)/shard_map/reduce_scatter | solution.py:37
  483.6 2.0 convolution_bitcast_fusion
  485.6 1.6 multiply_convert_fusion
  487.2 198.9 %all-reduce.3.cloned.1.call-done = f32[256,64]{0,1:T(8,128)} async-done(((f32[256,64]{0,1:T(8,128)}), f32[256,64]{0,1:T(8,128)}) %all-reduce.3.cloned.1.call-update) | async-done | bytes 65552
  686.1 0.8 dynamic-slice_subtract_fusion
  686.9 0.7 copy.17
  (20 shorter events, 0.3 us)
Async XLA Ops:
  7.2 82.2 %copy-start = (bf16[768,1536]{1,0:T(8,128)(2,1)S(1)}, bf16[768,1536]{1,0:T(8,128)(2,1)}, u32[]{:S(2)}) copy-start(bf16[768,1536]{1,0:T(8,128)(2,1)} %param.4) | copy-start | bytes 7077892
  7.2 74.5 %all-gather.4.cloned.1.call-start = ((), (), s32[]{:S(2)}) async-start(), calls=%async_computation.1 | async-start | bytes 3244032 | tf_op jit(solution)/shard_map/all_gather | solution.py:27
  7.9 372.2 %all-gather.6.cloned.1.call-start = ((), (), s32[]{:S(2)}) async-start(), calls=%async_computation.3 | async-start | bytes 26738688 | tf_op jit(solution)/shard_map/all_gather | solution.py:12
  86.0 1.8 copy-start.1
  89.3 394.2 %reduce-scatter.3.cloned.1.call-start = ((), (), s32[]{:S(2)}) async-start(), calls=%async_computation.2 | async-start | bytes 3342336 | tf_op jit(solution)/shard_map/reduce_scatter | solution.py:37
  95.7 0.7 copy-start.2
  95.7 1.1 copy-start.3
  95.7 590.3 %all-reduce.3.cloned.1.call-start = ((), (), s32[]{:S(2)}) async-start(), calls=%async_computation.4 | async-start | bytes 131072
Sparse Core Ops, SparseCore 0:
  10.1 71.4 all-gather.3
  89.5 290.6 all-gather.5
  384.3 99.1 reduce-scatter.2
  486.3 199.7 all-reduce.2
